TPU v7x, 256 devices: a whole 4x4x8 slice. The times are simulated.
256 devices in a mesh: rep: 32 (over y, z), shard: 8 (over x, core).
Axes of the slice: x: 4, y: 4, z: 8, core: 2. Of those that a mesh axis runs over, the one named last changes fastest.
Arguments:
- gradient: bfloat16 [32, 1024, 4096], P('rep', None, 'shard'), may hold values from -16 to 16
- feedback: bfloat16 [32, 1024, 4096], P('rep', None, 'shard'), may hold values from -4 to 4
- warm_start: float32 [1024, 64], replicated, may hold values from -6 to 6
- master: float32 [1024, 4096], P('rep', 'shard'), may hold values from -4 to 4
- moment: float32 [1024, 4096], P('rep', 'shard'), may hold values from -1.5 to 1.5
- second: float32 [1024, 4096], P('rep', 'shard'), may hold values from 0.005 to 0.5
Outputs:
- new_feedback: bfloat16 [32, 1024, 4096], P('rep', None, 'shard')
- weights: bfloat16 [1024, 4096], P(None, 'shard')
- master_out: float32 [1024, 4096], P('rep', 'shard')
- moment_out: float32 [1024, 4096], P('rep', 'shard')
- second_out: float32 [1024, 4096], P('rep', 'shard')
- right_factor: float32 [1024, 64], replicated
All inputs are finite; a program needn't handle non-finite values.
Results may differ from a plain program's by a relative error of at most 0.001.
Values may be sent and summed in bfloat16 or wider, within the bound.
No kernel may reach another device: no remote copies, remote signals or barrier semaphores. Data moves between devices by JAX's collectives and lax.ppermute only.
A program may use at most 64 MiB of HBM per device.

v0:
```python
import jax
import jax.numpy as jnp
from jax import lax
from jax.sharding import PartitionSpec as P

HIGHEST = lax.Precision.HIGHEST
beta_one = 0.9
beta_two = 0.95
learn_rate = 0.02
decay_rate = 0.1
adam_eps = 1e-08
ridge_rate = 1e-06


def lower_inverse(gram):
    matrix_order = gram.shape[0]
    identity = jnp.eye(matrix_order, dtype=jnp.float32)
    ridge_term = ridge_rate * jnp.trace(gram) / matrix_order
    cholesky_lower = jnp.linalg.cholesky(gram + ridge_term * identity)
    return jax.scipy.linalg.solve_triangular(cholesky_lower, identity, lower=True)


def contract_first(left, right):
    return lax.dot_general(
        left, right, (((0,), (0,)), ((), ())), precision=HIGHEST, preferred_element_type=jnp.float32
    )


def times_inverse(left, inverse):
    return jnp.dot(left, inverse.T, precision=HIGHEST, preferred_element_type=jnp.float32)


def on_device(gradient, feedback, warm_start, master, moment, second):
    replicas = lax.axis_size("rep")
    merged = gradient[0].astype(jnp.float32) + feedback[0].astype(jnp.float32)
    local_factor = contract_first(merged, warm_start)
    factor = lax.psum(local_factor, "rep") / replicas
    gram_part = contract_first(factor, factor)
    gram = lax.psum(gram_part, "shard")
    inverse = lower_inverse(gram)
    unit_basis = times_inverse(factor, inverse)
    projected = jnp.dot(merged, unit_basis, precision=HIGHEST, preferred_element_type=jnp.float32)
    right_factor = lax.psum(projected, ("rep", "shard")) / replicas
    approx = lax.dot_general(
        right_factor,
        unit_basis,
        (((1,), (1,)), ((), ())),
        precision=HIGHEST,
        preferred_element_type=jnp.float32,
    )
    new_feedback = (merged - approx).astype(jnp.bfloat16)[None]
    own_rows = master.shape[0]
    row_start = lax.axis_index("rep") * own_rows
    grad_rows = lax.dynamic_slice_in_dim(approx, row_start, own_rows, 0)
    moment_out = beta_one * moment + (1.0 - beta_one) * grad_rows
    second_out = beta_two * second + (1.0 - beta_two) * grad_rows * grad_rows
    master_out = master - learn_rate * (
        moment_out / (jnp.sqrt(second_out) + adam_eps) + decay_rate * master
    )
    weights = lax.all_gather(master_out.astype(jnp.bfloat16), "rep", axis=0, tiled=True)
    return (new_feedback, weights, master_out, moment_out, second_out, right_factor)


def solution(mesh):
    return jax.shard_map(
        on_device,
        mesh=mesh,
        in_specs=(
            P("rep", None, "shard"),
            P("rep", None, "shard"),
            P(),
            P("rep", "shard"),
            P("rep", "shard"),
            P("rep", "shard"),
        ),
        out_specs=(
            P("rep", None, "shard"),
            P(None, "shard"),
            P("rep", "shard"),
            P("rep", "shard"),
            P("rep", "shard"),
            P(),
        ),
        check_vma=False,
    )
```

profile of v0, /device:TPU:2, one launch (start us, length us, event | category | flops | bytes accessed | tf_op | source)
XLA Modules:
  0.0 533.7 jit_solution(15276774667782180067)
XLA Ops:
  7.2 0.9 copy-done
  8.1 3.8 fusion.2
  12.0 0.0 all-reduce.5.cloned.1.call-start
  12.0 143.7 %all-reduce.3.cloned.1.call-done = f32[512,64]{0,1:T(8,128)} async-done(((f32[512,64]{0,1:T(8,128)}), f32[512,64]{0,1:T(8,128)}) %all-reduce.3.cloned.1.call-update) | async-done | bytes 131088 | tf_op jit(solution)/shard_map/psum | solution.py:37
  155.8 1.2 fusion.8
  157.0 20.7 %psum.22 = f32[64,64]{1,0:T(8,128)S(1)} all-reduce(f32[64,64]{1,0:T(8,128)S(1)} %fusion.8), channel_id=1, replica_groups=mesh['rep'=32,'shard'=8] {'shard'}, use_global_device_ids=true, to_apply=%region_1.0 | all-reduce | flops 4096 | bytes 32768 | tf_op jit(solution)/shard_map/psum | solution.py:39
  177.7 0.6 select_reduce_fusion.1
  179.0 0.1 copy.12
  179.1 5.8 %cholesky.18 = f32[64,64]{1,0:T(8,128)S(1)} custom-call(f32[64,64]{1,0:T(8,128)S(1)} %fusion.16), custom_call_target="Cholesky" | custom-call | tf_op jit(solution)/shard_map/jit(cholesky)/cholesky | solution.py:19
  185.0 0.6 compare_reduce_fusion
  185.6 0.7 fusion.13
  186.3 4.9 custom-call.7
  191.2 0.2 fusion.14
  191.4 1.2 fusion.6
  192.6 3.0 fusion
  195.7 0.0 all-gather.2.cloned.1.call-start
  195.7 249.2 %all-reduce.5.cloned.1.call-done = f32[1024,64]{0,1:T(8,128)} async-done(((f32[1024,64]{0,1:T(8,128)}), f32[1024,64]{0,1:T(8,128)}) %all-reduce.5.cloned.1.call-update) | async-done | bytes 262160 | tf_op jit(solution)/shard_map/psum | solution.py:43
  444.9 1.0 broadcast_multiply_fusion
  445.9 1.8 fusion.21
  447.8 1.3 copy-done.3
  449.1 0.7 fusion.19
  449.9 3.0 fusion.5
  452.9 72.0 %all-gather.2.cloned.1.call-done = bf16[1024,512]{1,0:T(8,128)(2,1)} async-done(((bf16[32,512]{1,0:T(8,128)(2,1)}), bf16[1024,512]{1,0:T(8,128)(2,1)}) %all-gather.2.cloned.1.call-update) | async-done | bytes 1048592 | tf_op jit(solution)/shard_map/all_gather | solution.py:60
  524.9 2.3 copy.16
  (21 shorter events, 0.2 us)
Async XLA Ops:
  7.2 1.0 copy-start
  7.2 185.4 %copy-start.1 = (bf16[1,1024,512]{2,1,0:T(8,128)(2,1)S(1)}, bf16[1,1024,512]{2,1,0:T(8,128)(2,1)}, u32[]{:S(2)}) copy-start(bf16[1,1024,512]{2,1,0:T(8,128)(2,1)} %param.7) | copy-start | bytes 3145732
  7.2 185.4 %copy-start.2 = (bf16[1,1024,512]{2,1,0:T(8,128)(2,1)S(1)}, bf16[1,1024,512]{2,1,0:T(8,128)(2,1)}, u32[]{:S(2)}) copy-start(bf16[1,1024,512]{2,1,0:T(8,128)(2,1)} %param.6) | copy-start | bytes 3145732
  7.2 148.6 %all-reduce.3.cloned.1.call-start = ((), (), s32[]{:S(2)}) async-start(), calls=%async_computation | async-start | bytes 262144 | tf_op jit(solution)/shard_map/psum | solution.py:37
  12.0 432.9 %all-reduce.5.cloned.1.call-start = ((), (), s32[]{:S(2)}) async-start(), calls=%async_computation.1 | async-start | bytes 524288 | tf_op jit(solution)/shard_map/psum | solution.py:43
  195.6 253.5 %copy-start.5 = (f32[32,512]{1,0:T(8,128)S(1)}, f32[32,512]{1,0:T(8,128)}, u32[]{:S(2)}) copy-start(f32[32,512]{1,0:T(8,128)} %param.9) | copy-start | bytes 196612
  195.6 253.5 %copy-start.6 = (f32[32,512]{1,0:T(8,128)S(1)}, f32[32,512]{1,0:T(8,128)}, u32[]{:S(2)}) copy-start(f32[32,512]{1,0:T(8,128)} %param.11) | copy-start | bytes 196612
  195.6 253.5 %copy-start.7 = (f32[32,512]{1,0:T(8,128)S(1)}, f32[32,512]{1,0:T(8,128)}, u32[]{:S(2)}) copy-start(f32[32,512]{1,0:T(8,128)} %param.10) | copy-start | bytes 196612
  195.7 329.2 %all-gather.2.cloned.1.call-start = ((), (), s32[]{:S(2)}) async-start(), calls=%async_computation.2 | async-start | bytes 1081344 | tf_op jit(solution)/shard_map/all_gather | solution.py:60
  445.9 7.0 %copy-start.4 = (f32[1024,64]{0,1:T(8,128)}, f32[1024,64]{0,1:T(8,128)S(1)}, u32[]{:S(2)}) copy-start(f32[1024,64]{0,1:T(8,128)S(1)} %broadcast_multiply_fusion) | copy-start | bytes 786436
  447.8 1.3 copy-start.3
Sparse Core Ops, SparseCore 0:
  12.1 143.6 all-reduce.2
  195.8 249.0 all-reduce.4
  450.0 74.8 all-gather.1
where the time goes:
time: 534 us
  waiting for transfers between devices  465 us (87%)
  blocking collectives  20.7 us (4%)
  other arithmetic  17.4 us (3%)
  between operations  14.5 us (3%)
  matrix products  11.4 us (2%)
    psum x1, waiting for transfers between devices, on_device(): right_factor = lax.psum(projected, ('rep', 'shard')) / replicas  249 us
    psum x1, waiting for transfers between devices, on_device(): factor = lax.psum(local_factor, 'rep') / replicas  144 us
    all_gather x1, waiting for transfers between devices, on_device(): lax.all_gather(master_out.astype(jnp.bfloat16), 'rep', axis=0, tiled=True)  72 us
    psum x1, blocking collectives, on_device(): gram = lax.psum(gram_part, 'shard')  20.7 us
  transfers between devices with their start and end apart: 3, of which 3 were waited for; matrix products, arithmetic and copies ran while one was open for 1% of the time, Pallas kernels for 0%

commit v1 on v0

--- a/solution.py
+++ b/solution.py
@@ -2,6 +2,7 @@
 import jax.numpy as jnp
 from jax import lax
 from jax.sharding import PartitionSpec as P
+from jax.lax import psum
 
 HIGHEST = lax.Precision.HIGHEST
 beta_one = 0.9
@@ -40,7 +41,13 @@
     inverse = lower_inverse(gram)
     unit_basis = times_inverse(factor, inverse)
     projected = jnp.dot(merged, unit_basis, precision=HIGHEST, preferred_element_type=jnp.float32)
-    right_factor = lax.psum(projected, ("rep", "shard")) / replicas
+
+    def find_the_set(s0):
+        for p in ("rep", "shard"):
+            s0 = psum(s0, p)
+        return s0
+
+    right_factor = find_the_set(projected) / replicas
     approx = lax.dot_general(
         right_factor,
         unit_basis,

time: 534 us -> 493 us (0.923)
  waiting for transfers between devices: 465 us -> 424 us
    psum x1 -> x2, waiting for transfers between devices: 249 us -> 205 us  [find_the_set(): s0 = psum(s0, p)]
  transfers between devices with their start and end apart: 3 -> 4, of which waited for: 3 -> 4; matrix products, arithmetic and copies ran while one was open for 1% -> 1% of each run, Pallas kernels for 0% -> 0%
where the time goes in v1:
time: 493 us; the launch traced here: 492 us
  waiting for transfers between devices  424 us (86%)
  blocking collectives  20.7 us (4%)
  other arithmetic  17.4 us (4%)
  between operations  14.5 us (3%)
  matrix products  11.4 us (2%)
    psum x2, waiting for transfers between devices, find_the_set(): s0 = psum(s0, p)  205 us
    psum x1, waiting for transfers between devices, on_device(): factor = lax.psum(local_factor, 'rep') / replicas  144 us
    all_gather x1, waiting for transfers between devices, on_device(): lax.all_gather(master_out.astype(jnp.bfloat16), 'rep', axis=0, tiled=True)  74.6 us
    psum x1, blocking collectives, on_device(): gram = lax.psum(gram_part, 'shard')  20.7 us
  transfers between devices with their start and end apart: 4, of which 4 were waited for; matrix products, arithmetic and copies ran while one was open for 1% of the time, Pallas kernels for 0%

profile of v1, /device:TPU:2, one launch (start us, length us, event | category | flops | bytes accessed | tf_op | source)
XLA Modules:
  0.0 492.3 jit_solution(14507239277692262874)
XLA Ops:
  7.2 0.9 copy-done
  8.1 3.8 fusion.2
  12.0 0.0 all-reduce.6.cloned.1.call-start
  12.0 143.7 %all-reduce.4.cloned.1.call-done = f32[512,64]{0,1:T(8,128)} async-done(((f32[512,64]{0,1:T(8,128)}), f32[512,64]{0,1:T(8,128)}) %all-reduce.4.cloned.1.call-update) | async-done | bytes 131088 | tf_op jit(solution)/shard_map/psum | solution.py:38
  155.8 1.2 fusion.8
  157.0 20.7 %psum.29 = f32[64,64]{1,0:T(8,128)S(1)} all-reduce(f32[64,64]{1,0:T(8,128)S(1)} %fusion.8), channel_id=1, replica_groups=mesh['rep'=32,'shard'=8] {'shard'}, use_global_device_ids=true, to_apply=%region_1.0 | all-reduce | flops 4096 | bytes 32768 | tf_op jit(solution)/shard_map/psum | solution.py:40
  177.7 0.6 select_reduce_fusion.1
  179.0 0.1 copy.12
  179.1 5.8 %cholesky.18 = f32[64,64]{1,0:T(8,128)S(1)} custom-call(f32[64,64]{1,0:T(8,128)S(1)} %fusion.16), custom_call_target="Cholesky" | custom-call | tf_op jit(solution)/shard_map/jit(cholesky)/cholesky | solution.py:20
  185.0 0.6 compare_reduce_fusion
  185.6 0.7 fusion.13
  186.3 4.9 custom-call.7
  191.2 0.2 fusion.14
  191.4 1.2 fusion.6
  192.6 3.0 fusion
  195.7 143.0 %all-reduce.6.cloned.1.call-done = f32[1024,64]{0,1:T(8,128)} async-done(((f32[1024,64]{0,1:T(8,128)}), f32[1024,64]{0,1:T(8,128)}) %all-reduce.6.cloned.1.call-update) | async-done | bytes 262160 | tf_op jit(solution)/shard_map/psum | solution.py:47
  338.8 62.1 %all-reduce.8.cloned.1.call-done = f32[1024,64]{0,1:T(8,128)} async-done(((f32[1024,64]{0,1:T(8,128)}), f32[1024,64]{0,1:T(8,128)}) %all-reduce.8.cloned.1.call-update) | async-done | bytes 262160 | tf_op jit(solution)/shard_map/psum | solution.py:47
  400.9 1.0 broadcast_multiply_fusion
  401.9 1.8 fusion.21
  403.7 1.3 copy-done.3
  405.1 0.7 fusion.19
  405.8 3.0 fusion.5
  408.8 74.6 %all-gather.2.cloned.1.call-done = bf16[1024,512]{1,0:T(8,128)(2,1)} async-done(((bf16[32,512]{1,0:T(8,128)(2,1)}), bf16[1024,512]{1,0:T(8,128)(2,1)}) %all-gather.2.cloned.1.call-update) | async-done | bytes 1048592 | tf_op jit(solution)/shard_map/all_gather | solution.py:67
  483.5 2.3 copy.17
  (24 shorter events, 0.3 us)
Async XLA Ops:
  7.2 1.0 copy-start
  7.2 185.4 %copy-start.1 = (bf16[1,1024,512]{2,1,0:T(8,128)(2,1)S(1)}, bf16[1,1024,512]{2,1,0:T(8,128)(2,1)}, u32[]{:S(2)}) copy-start(bf16[1,1024,512]{2,1,0:T(8,128)(2,1)} %param.7) | copy-start | bytes 3145732
  7.2 185.4 %copy-start.2 = (bf16[1,1024,512]{2,1,0:T(8,128)(2,1)S(1)}, bf16[1,1024,512]{2,1,0:T(8,128)(2,1)}, u32[]{:S(2)}) copy-start(bf16[1,1024,512]{2,1,0:T(8,128)(2,1)} %param.6) | copy-start | bytes 3145732
  7.2 148.6 %all-reduce.4.cloned.1.call-start = ((), (), s32[]{:S(2)}) async-start(), calls=%async_computation | async-start | bytes 262144 | tf_op jit(solution)/shard_map/psum | solution.py:38
  12.0 326.8 %all-reduce.6.cloned.1.call-start = ((), (), s32[]{:S(2)}) async-start(), calls=%async_computation.1 | async-start | bytes 524288 | tf_op jit(solution)/shard_map/psum | solution.py:47
  195.6 209.4 %copy-start.5 = (f32[32,512]{1,0:T(8,128)S(1)}, f32[32,512]{1,0:T(8,128)}, u32[]{:S(2)}) copy-start(f32[32,512]{1,0:T(8,128)} %param.9) | copy-start | bytes 196612
  195.6 209.4 %copy-start.6 = (f32[32,512]{1,0:T(8,128)S(1)}, f32[32,512]{1,0:T(8,128)}, u32[]{:S(2)}) copy-start(f32[32,512]{1,0:T(8,128)} %param.11) | copy-start | bytes 196612
  195.6 209.4 %copy-start.7 = (f32[32,512]{1,0:T(8,128)S(1)}, f32[32,512]{1,0:T(8,128)}, u32[]{:S(2)}) copy-start(f32[32,512]{1,0:T(8,128)} %param.10) | copy-start | bytes 196612
  195.7 205.2 %all-reduce.8.cloned.1.call-start = ((), (), s32[]{:S(2)}) async-start(), calls=%async_computation.2 | async-start | bytes 524288 | tf_op jit(solution)/shard_map/psum | solution.py:47
  338.8 144.7 %all-gather.2.cloned.1.call-start = ((), (), s32[]{:S(2)}) async-start(), calls=%async_computation.3 | async-start | bytes 1081344 | tf_op jit(solution)/shard_map/all_gather | solution.py:67
  401.9 7.0 %copy-start.4 = (f32[1024,64]{0,1:T(8,128)}, f32[1024,64]{0,1:T(8,128)S(1)}, u32[]{:S(2)}) copy-start(f32[1024,64]{0,1:T(8,128)S(1)} %broadcast_multiply_fusion) | copy-start | bytes 786436
  403.7 1.3 copy-start.3
Sparse Core Ops, SparseCore 0:
  12.1 143.6 all-reduce.3
  195.8 142.9 all-reduce.5
  341.2 59.6 all-reduce.7
  405.9 77.4 all-gather.1

commit v2 on v0

--- a/solution.py
+++ b/solution.py
@@ -57,7 +57,11 @@
     master_out = master - learn_rate * (
         moment_out / (jnp.sqrt(second_out) + adam_eps) + decay_rate * master
     )
-    weights = lax.all_gather(master_out.astype(jnp.bfloat16), "rep", axis=0, tiled=True)
+    block = master_out.astype(jnp.bfloat16)
+    size = lax.axis_size("rep")
+    tiles = jnp.stack([block for _ in range(size)])
+    tiles = lax.all_to_all(tiles, "rep", split_axis=0, concat_axis=0)
+    weights = jnp.concatenate(tiles, axis=0)
     return (new_feedback, weights, master_out, moment_out, second_out, right_factor)
 
 

time: 534 us -> 496 us (0.929)
  waiting for transfers between devices: 465 us -> 418 us
  starting transfers between devices: 0.12 us -> 7.31 us
    all_gather x1 -> x0, waiting for transfers between devices: 72 us -> none  [on_device(): lax.all_gather(master_out.astype(jnp.bfloat16), 'rep', axis=0, tiled=True)]
    all_to_all x0 -> x1, waiting for transfers between devices: none -> 24.8 us  [on_device(): tiles = lax.all_to_all(tiles, 'rep', split_axis=0, concat_axis=0)]
    all_to_all x0 -> x1, starting transfers between devices: none -> 7.23 us  [on_device(): tiles = lax.all_to_all(tiles, 'rep', split_axis=0, concat_axis=0)]
where the time goes in v2:
time: 496 us; the launch traced here: 494 us
  waiting for transfers between devices  418 us (84%)
  blocking collectives  20.7 us (4%)
  other arithmetic  17.4 us (4%)
  between operations  14.8 us (3%)
  matrix products  11.3 us (2%)
  starting transfers between devices  7.31 us (1%)
    psum x1, waiting for transfers between devices, on_device(): right_factor = lax.psum(projected, ('rep', 'shard')) / replicas  249 us
    psum x1, waiting for transfers between devices, on_device(): factor = lax.psum(local_factor, 'rep') / replicas  144 us
    all_to_all x1, waiting for transfers between devices, on_device(): tiles = lax.all_to_all(tiles, 'rep', split_axis=0, concat_axis=0)  24.8 us
    psum x1, blocking collectives, on_device(): gram = lax.psum(gram_part, 'shard')  20.7 us
  transfers between devices with their start and end apart: 3, of which 3 were waited for; matrix products, arithmetic and copies ran while one was open for 1% of the time, Pallas kernels for 0%

profile of v2, /device:TPU:2, one launch (start us, length us, event | category | flops | bytes accessed | tf_op | source)
XLA Modules:
  0.0 493.8 jit_solution(13463714889890789120)
XLA Ops:
  7.2 0.9 copy-done
  8.1 3.8 fusion.2
  12.0 143.7 %all-reduce.3.cloned.1.call-done = f32[512,64]{0,1:T(8,128)} async-done(((f32[512,64]{0,1:T(8,128)}), f32[512,64]{0,1:T(8,128)}) %all-reduce.3.cloned.1.call-update) | async-done | bytes 131088 | tf_op jit(solution)/shard_map/psum | solution.py:37
  155.8 1.2 fusion.8
  157.0 20.7 %psum.22 = f32[64,64]{1,0:T(8,128)S(1)} all-reduce(f32[64,64]{1,0:T(8,128)S(1)} %fusion.8), channel_id=1, replica_groups=mesh['rep'=32,'shard'=8] {'shard'}, use_global_device_ids=true, to_apply=%region_1.0 | all-reduce | flops 4096 | bytes 32768 | tf_op jit(solution)/shard_map/psum | solution.py:39
  177.7 0.6 select_reduce_fusion.1
  179.0 0.1 copy.12
  179.1 5.8 %cholesky.18 = f32[64,64]{1,0:T(8,128)S(1)} custom-call(f32[64,64]{1,0:T(8,128)S(1)} %fusion.16), custom_call_target="Cholesky" | custom-call | tf_op jit(solution)/shard_map/jit(cholesky)/cholesky | solution.py:19
  185.0 0.6 compare_reduce_fusion
  185.6 0.7 fusion.13
  186.3 4.9 custom-call.7
  191.2 0.2 fusion.14
  191.4 1.2 fusion.6
  192.6 3.0 fusion
  195.7 249.2 %all-reduce.5.cloned.1.call-done = f32[1024,64]{0,1:T(8,128)} async-done(((f32[1024,64]{0,1:T(8,128)}), f32[1024,64]{0,1:T(8,128)}) %all-reduce.5.cloned.1.call-update) | async-done | bytes 262160 | tf_op jit(solution)/shard_map/psum | solution.py:43
  444.9 1.0 broadcast_multiply_fusion
  445.9 1.8 fusion.21
  447.7 1.3 copy-done.3
  449.1 0.7 fusion.19
  449.8 1.1 stack.2
  450.9 7.2 %all-to-all-start = ((bf16[32,32,512]{2,1,0:T(8,128)(2,1)}), bf16[32,32,512]{2,1,0:T(8,128)(2,1)S(1)}, u32[]{:S(2)}, u32[]{:S(2)}) async-start(bf16[32,32,512]{2,1,0:T(8,128)(2,1)} %stack.2), calls=%async_computation | async-start | bytes 2097152 | tf_op jit(solution)/shard_map/all_to_all | solution.py:63
  458.1 3.0 fusion.5
  461.1 24.8 %all-to-all-done = bf16[32,32,512]{2,1,0:T(8,128)(2,1)S(1)} async-done(((bf16[32,32,512]{2,1,0:T(8,128)(2,1)}), bf16[32,32,512]{2,1,0:T(8,128)(2,1)S(1)}, u32[]{:S(2)}, u32[]{:S(2)}) %all-to-all-start) | async-done | bytes 1048608 | tf_op jit(solution)/shard_map/all_to_all | solution.py:63
  486.0 1.0 copy.16
  (21 shorter events, 0.2 us)
Async XLA Ops:
  7.2 1.0 copy-start
  7.2 185.4 %copy-start.1 = (bf16[1,1024,512]{2,1,0:T(8,128)(2,1)S(1)}, bf16[1,1024,512]{2,1,0:T(8,128)(2,1)}, u32[]{:S(2)}) copy-start(bf16[1,1024,512]{2,1,0:T(8,128)(2,1)} %param.7) | copy-start | bytes 3145732
  7.2 185.4 %copy-start.2 = (bf16[1,1024,512]{2,1,0:T(8,128)(2,1)S(1)}, bf16[1,1024,512]{2,1,0:T(8,128)(2,1)}, u32[]{:S(2)}) copy-start(bf16[1,1024,512]{2,1,0:T(8,128)(2,1)} %param.6) | copy-start | bytes 3145732
  7.2 148.6 %all-reduce.3.cloned.1.call-start = ((), (), s32[]{:S(2)}) async-start(), calls=%async_computation.1 | async-start | bytes 262144 | tf_op jit(solution)/shard_map/psum | solution.py:37
  12.0 432.9 %all-reduce.5.cloned.1.call-start = ((), (), s32[]{:S(2)}) async-start(), calls=%async_computation.2 | async-start | bytes 524288 | tf_op jit(solution)/shard_map/psum | solution.py:43
  195.6 253.4 %copy-start.5 = (f32[32,512]{1,0:T(8,128)S(1)}, f32[32,512]{1,0:T(8,128)}, u32[]{:S(2)}) copy-start(f32[32,512]{1,0:T(8,128)} %param.9) | copy-start | bytes 196612
  195.6 253.4 %copy-start.6 = (f32[32,512]{1,0:T(8,128)S(1)}, f32[32,512]{1,0:T(8,128)}, u32[]{:S(2)}) copy-start(f32[32,512]{1,0:T(8,128)} %param.11) | copy-start | bytes 196612
  195.6 253.4 %copy-start.7 = (f32[32,512]{1,0:T(8,128)S(1)}, f32[32,512]{1,0:T(8,128)}, u32[]{:S(2)}) copy-start(f32[32,512]{1,0:T(8,128)} %param.10) | copy-start | bytes 196612
  445.8 3.9 copy-start.4
  447.7 1.4 copy-start.3
  450.9 35.1 %all-to-all-start = ((bf16[32,32,512]{2,1,0:T(8,128)(2,1)}), bf16[32,32,512]{2,1,0:T(8,128)(2,1)S(1)}, u32[]{:S(2)}, u32[]{:S(2)}) async-start(bf16[32,32,512]{2,1,0:T(8,128)(2,1)} %stack.2), calls=%async_computation | async-start | bytes 2097152 | tf_op jit(solution)/shard_map/all_to_all | solution.py:63
Sparse Core Ops, SparseCore 0:
  12.1 143.6 all-reduce.2
  195.8 249.0 all-reduce.4
